TPU v7x, 512 devices: a whole 4x4x16 slice. The times are simulated.
512 devices in a mesh: tm: 64 (over y, z), head: 8 (over x, core).
Axes of the slice: x: 4, y: 4, z: 16, core: 2. Of those that a mesh axis runs over, the one named last changes fastest.
Arguments:
- frames: bfloat16 [16384, 1024], P('tm'), may hold values from -6 to 6
- x_weight: bfloat16 [1024, 2048], P('tm', 'head'), may hold values from -0.1875 to 0.1875
- z_weight: bfloat16 [1024, 2048], P('tm', 'head'), may hold values from -0.1875 to 0.1875
- bc_weight: bfloat16 [1024, 256], P('tm'), may hold values from -0.1875 to 0.1875
- log_decay: float32 [32, 16384], P('head', 'tm'), may hold values from -0.9 to 0
- norm_gain: float32 [2048], P('head'), may hold values from 0.1 to 1.9
- conv_weight: float32 [31, 2048], P(None, 'head'), may hold values from -1 to 1
- out_weight: bfloat16 [2048, 1024], P('head', 'tm'), may hold values from -0.125 to 0.125
- record_lengths: int32 [8], replicated, may hold values from 1 to 12288, 16384 in all
Outputs:
- mixed: bfloat16 [16384, 1024], P('tm', 'head')
Inputs may be any that keep to these rules, and one draw needn't show every extreme that they name: `record_lengths`: 8 recording lengths that sum to 16384; the longest has exactly 12288 frames.
All inputs are finite; a program needn't handle non-finite values.
Results may differ from a plain program's by a relative error of at most 0.02.
Values may be sent and summed in bfloat16 or wider, within the bound.
A program may use at most 64 MiB of HBM per device.

v0:
```python
import jax
import jax.numpy as jnp
from jax import lax
from jax.sharding import PartitionSpec as P

SPAN = 128
highest = lax.Precision.HIGHEST


def extended_2(array, sides, width):
    for axis, dim in sides:
        peers, length = (lax.axis_size(axis), array.shape[dim])
        up = [(i, (i + 1) % peers) for i in range(peers - 1)]
        down = [(j, i) for i, j in up]
        last = lax.slice_in_dim(array, length - width, length, axis=dim)
        leading = lax.slice_in_dim(array, 0, width, axis=dim)
        before = lax.ppermute(last, axis, up)
        after = lax.ppermute(leading, axis, down)
        array = jnp.concatenate([before, array, after], axis=dim)
    return array


def segment_ids(record_lengths, positions):
    record_ends = jnp.cumsum(record_lengths)
    return jnp.sum((record_ends[None, :] <= positions[:, None]).astype(jnp.int32), axis=1)


def span_step(state, inputs):
    x_block, b_block, c_block, log_block, seg_block, seg_before = inputs
    length = seg_block.shape[0]
    cumul = jnp.cumsum(log_block, axis=1)
    lower = jnp.arange(length)[:, None] >= jnp.arange(length)[None, :]
    joined = (seg_block[:, None] == seg_block[None, :]) & lower
    spread = cumul[:, :, None] - cumul[:, None, :]
    mixing = jnp.exp(jnp.where(joined[None], spread, -jnp.inf))
    scores = jnp.dot(c_block, b_block.T, preferred_element_type=jnp.float32)
    x_float = x_block.astype(jnp.float32)
    inner = jnp.einsum("hts,shp->thp", mixing * scores[None], x_float, precision=highest)
    carried = jnp.exp(cumul) * (seg_block == seg_before).astype(jnp.float32)[None, :]
    c_float = c_block.astype(jnp.float32)
    outer = jnp.einsum("tn,hnp->thp", c_float, state, precision=highest) * carried.T[:, :, None]
    tail = (
        jnp.exp(cumul[:, -1:] - cumul) * (seg_block == seg_block[-1]).astype(jnp.float32)[None, :]
    )
    weighted = tail[:, :, None] * b_block.astype(jnp.float32)[None, :, :]
    state_next = carried[:, -1][:, None, None] * state + jnp.einsum(
        "hsn,shp->hnp", weighted, x_float, precision=highest
    )
    return (state_next, inner + outer)


def run_spans(x_rows, b_rows, c_rows, log_rows, seg_rows, seg_first, state):
    count = x_rows.shape[0] // SPAN
    heads_here = log_rows.shape[0]
    x_blocks = x_rows.reshape(count, SPAN, heads_here, -1)
    b_blocks = b_rows.reshape(count, SPAN, -1)
    c_blocks = c_rows.reshape(count, SPAN, -1)
    log_blocks = log_rows.reshape(heads_here, count, SPAN).transpose(1, 0, 2)
    seg_blocks = seg_rows.reshape(count, SPAN)
    seg_befores = jnp.concatenate([jnp.reshape(seg_first, (1,)), seg_blocks[:-1, -1]])
    state, outputs = lax.scan(
        span_step, state, (x_blocks, b_blocks, c_blocks, log_blocks, seg_blocks, seg_befores)
    )
    return (state, outputs.reshape(count * SPAN, heads_here, -1))


def gate_rows(ssd_out, z_rows, norm_gain):
    square_mean = jnp.mean(ssd_out * ssd_out, axis=-1, keepdims=True)
    normed = (ssd_out * lax.rsqrt(square_mean + 1e-05)).reshape(ssd_out.shape[0], -1)
    z_float = z_rows.astype(jnp.float32)
    return (normed * norm_gain[None, :] * z_float * jax.nn.sigmoid(z_float)).astype(jnp.bfloat16)


def conv_rows(extended, seg_extended, seg_rows, conv_weight):
    frame_count = seg_rows.shape[0]
    summed = jnp.zeros((frame_count, extended.shape[1]), jnp.float32)
    for offset in range(conv_weight.shape[0]):
        same = (seg_extended[offset : offset + frame_count] == seg_rows).astype(jnp.float32)
        summed = (
            summed
            + conv_weight[offset][None, :]
            * extended[offset : offset + frame_count].astype(jnp.float32)
            * same[:, None]
        )
    return (summed * jax.nn.sigmoid(summed)).astype(jnp.bfloat16)


def local(
    frames,
    x_weight,
    z_weight,
    bc_weight,
    log_decay,
    norm_gain,
    conv_weight,
    out_weight,
    record_lengths,
):
    frame_count = frames.shape[0]
    state_width = bc_weight.shape[1] // 2
    pieces = (
        lax.all_gather(x_weight, "tm", axis=0, tiled=True),
        lax.all_gather(z_weight, "tm", axis=0, tiled=True),
        lax.all_gather(bc_weight, "tm", axis=0, tiled=True),
    )
    x_sum, z_sum, bc_sum = tuple(
        (jnp.dot(frames, weight_rows, preferred_element_type=jnp.float32) for weight_rows in pieces)
    )
    bc_rows = bc_sum.astype(jnp.bfloat16)
    x_rows = x_sum.astype(jnp.bfloat16)
    z_rows = z_sum.astype(jnp.bfloat16)
    dev_start = lax.axis_index("tm") * frame_count
    positions = dev_start + jnp.arange(frame_count, dtype=jnp.int32)
    seg_rows = segment_ids(record_lengths, positions)
    seg_before_dev = segment_ids(record_lengths, jnp.reshape(dev_start - 1, (1,)))[0]
    seg_first = jnp.where(dev_start == 0, -1, seg_before_dev)
    heads_here = log_decay.shape[0]
    head_size = x_weight.shape[1] // heads_here
    empty_state = jnp.zeros((heads_here, state_width, head_size), jnp.float32)
    local_state, local_out = run_spans(
        x_rows,
        bc_rows[:, :state_width],
        bc_rows[:, state_width:],
        log_decay,
        seg_rows,
        seg_first,
        empty_state,
    )
    same_first = (seg_rows == seg_first).astype(jnp.float32)
    through = jnp.exp(jnp.sum(log_decay, axis=1)) * same_first[-1]
    all_keep, all_summaries = (
        lax.all_gather(through[None], "tm", axis=0, tiled=True),
        lax.all_gather(local_state[None], "tm", axis=0, tiled=True),
    )
    dev_index = lax.axis_index("tm")

    def absorb(position, carry_state):
        updated = all_keep[position][:, None, None] * carry_state + all_summaries[position]
        return jnp.where(position < dev_index, updated, carry_state)

    entry_state = lax.fori_loop(0, all_keep.shape[0], absorb, empty_state)
    growth = jnp.exp(jnp.cumsum(log_decay, axis=1)) * same_first[None, :]
    carried = (
        jnp.einsum(
            "tn,hnp->thp",
            bc_rows[:, state_width:].astype(jnp.float32),
            entry_state,
            precision=highest,
        )
        * growth.T[:, :, None]
    )
    ssd_out = local_out + carried
    gated = gate_rows(ssd_out, z_rows, norm_gain)
    half_width = (conv_weight.shape[0] - 1) // 2
    extended = extended_2(gated, (("tm", 0),), half_width)
    seg_extended = segment_ids(
        record_lengths,
        dev_start - half_width + jnp.arange(frame_count + 2 * half_width, dtype=jnp.int32),
    )
    act_rows = conv_rows(extended, seg_extended, seg_rows, conv_weight)
    partial_terms = jnp.dot(
        act_rows,
        lax.all_gather(out_weight, "tm", axis=1, tiled=True),
        preferred_element_type=jnp.float32,
    )
    return lax.psum_scatter(
        partial_terms.astype(jnp.bfloat16), "head", scatter_dimension=1, tiled=True
    )


def solution(mesh):
    in_specs = (
        P("tm", None),
        P("tm", "head"),
        P("tm", "head"),
        P("tm", None),
        P("head", "tm"),
        P("head"),
        P(None, "head"),
        P("head", "tm"),
        P(),
    )
    out_specs = P("tm", "head")
    return jax.shard_map(local, mesh=mesh, in_specs=in_specs, out_specs=out_specs, check_vma=False)
```

profile of v0, /device:TPU:8, one launch (start us, length us, event | category | flops | bytes accessed | tf_op | source)
XLA Modules:
  0.0 708.7 jit_solution(988738983611834852)
XLA Ops:
  8.9 106.5 %all_gather.18 = bf16[1024,256]{1,0:T(8,128)(2,1)S(1)} all-gather(bf16[16,256]{1,0:T(8,128)(2,1)} %param.16), channel_id=1, replica_groups=mesh['tm'=64,'head'=8] {'tm'}, dimensions={0}, use_global_device_ids=true | all-gather | bytes 532480 | tf_op jit(solution)/shard_map/all_gather | solution.py:104
  115.8 98.0 %all_gather.19 = bf16[1024,256]{1,0:T(8,128)(2,1)S(1)} all-gather(bf16[16,256]{1,0:T(8,128)(2,1)} %param.14), channel_id=1, replica_groups=mesh['tm'=64,'head'=8] {'tm'}, dimensions={0}, use_global_device_ids=true | all-gather | bytes 532480 | tf_op jit(solution)/shard_map/all_gather | solution.py:102
  215.9 16.3 %while.27 = (s32[]{:T(128)}, f32[4,128,64]{1,2,0:T(8,128)S(1)}, f32[2,128,4,64]{1,0,3,2:T(2,128)S(1)}, f32[2,4,128]{2,1,0:T(4,128)}, s32[2,128]{1,0:T(2,128)S(1)...) while((s32[]{:T(128)}, f32[4,128,64]{1,2,0:T(8,128)S(1)}, ...), condition=%wide.region_5.6_spmd.clone, body=%wide.region_3.5_spmd.clone.sunk | while | flops 155747840 | bytes 1896203 | solution.py:61
  220.8 2.6 dynamic_update_slice.6
  229.0 2.6 dynamic_update_slice.6
  234.5 1.3 dynamic-slice
  237.3 121.9 %all-reduce = f32[256]{0:T(256)S(1)} all-reduce(f32[256]{0:T(256)S(1)} %multiply_dynamic-update-slice_fusion), channel_id=2, replica_groups=mesh['tm'=64,'head'=8] {'tm'}, use_global_device_ids=true, to_apply=%add | all-reduce | flops 256 | bytes 2048
  360.0 1.2 reduce-window.11
  361.8 118.6 %all_gather.22 = bf16[1024,256]{1,0:T(8,128)(2,1)S(1)} all-gather(bf16[16,256]{1,0:T(8,128)(2,1)S(1)} %copy-done.3), channel_id=1, replica_groups=mesh['tm'=64,'head'=8] {'tm'}, dimensions={0}, use_global_device_ids=true | all-gather | bytes 532480 | tf_op jit(solution)/shard_map/all_gather | solution.py:103
  480.6 77.0 %while.28 = (s32[]{:T(128)}, f32[4,128,64]{2,1,0:T(8,128)S(1)}, s32[]{:T(128)}, f32[64,4]{1,0:T(8,128)S(1)}, f32[64,4,128,64]{2,3,1,0:T(8,128)}, /*index=5*/s32[]{:T(128)}, s32[]{:T(128)}) while((s32[]{:T(128)}, f32[4,128,64]{2,1,0:T(8,128)S(1)}, s32[]{:T(128)}, f32[64,4]{1,0:T(8,128)S(1)}, f32[64,4,128,64]{2,3,1,0:T(8,128)}, ...), condition=%wide.region_8.9_spmd.clone, body=%wide.region_7.8_spmd.clone.sunk | while | flops 131076 | bytes 917657 | solution.py:141
  484.2 0.9 constant_dynamic-slice_fusion.4
  485.5 0.9 constant_dynamic-slice_fusion.4
  486.7 0.9 constant_dynamic-slice_fusion.4
  487.9 0.9 constant_dynamic-slice_fusion.4
  489.1 0.9 constant_dynamic-slice_fusion.4
  490.3 0.9 constant_dynamic-slice_fusion.4
  491.5 0.9 constant_dynamic-slice_fusion.4
  495.1 0.9 constant_dynamic-slice_fusion.4
  496.3 0.9 constant_dynamic-slice_fusion.4
  497.5 0.9 constant_dynamic-slice_fusion.4
  498.7 0.9 constant_dynamic-slice_fusion.4
  499.9 0.9 constant_dynamic-slice_fusion.4
  501.1 0.9 constant_dynamic-slice_fusion.4
  502.3 0.9 constant_dynamic-slice_fusion.4
  507.1 0.9 constant_dynamic-slice_fusion.4
  508.3 0.9 constant_dynamic-slice_fusion.4
  509.5 0.9 constant_dynamic-slice_fusion.4
  510.7 0.9 constant_dynamic-slice_fusion.4
  511.9 0.9 constant_dynamic-slice_fusion.4
  513.1 0.9 constant_dynamic-slice_fusion.4
  514.3 0.9 constant_dynamic-slice_fusion.4
  517.9 0.9 constant_dynamic-slice_fusion.4
  519.1 0.9 constant_dynamic-slice_fusion.4
  520.3 0.9 constant_dynamic-slice_fusion.4
  521.5 0.9 constant_dynamic-slice_fusion.4
  522.7 0.9 constant_dynamic-slice_fusion.4
  524.0 0.9 constant_dynamic-slice_fusion.4
  525.2 0.9 constant_dynamic-slice_fusion.4
  530.0 0.9 constant_dynamic-slice_fusion.4
  531.2 0.9 constant_dynamic-slice_fusion.4
  532.4 0.9 constant_dynamic-slice_fusion.4
  558.6 1.9 collective-permute-start
  560.5 6.0 collective-permute-start.1
  566.6 96.8 %all_gather.23 = bf16[256,1024]{0,1:T(8,128)(2,1)S(1)} all-gather(bf16[256,16]{0,1:T(8,128)(2,1)S(1)} %copy-done.4), channel_id=1, replica_groups=mesh['tm'=64,'head'=8] {'tm'}, dimensions={1}, use_global_device_ids=true | all-gather | bytes 532480 | tf_op jit(solution)/shard_map/all_gather | solution.py:163
  663.3 3.0 convolution_convert_fusion
  666.4 1.0 copy.47
  667.4 32.9 %reduce-scatter.4.cloned.1.call-done = bf16[128,256]{1,0:T(8,128)(2,1)} async-done(((bf16[1024,256]{1,0:T(8,128)(2,1)}), bf16[128,256]{1,0:T(8,128)(2,1)}) %reduce-scatter.4.cloned.1.call-update) | async-done | bytes 65552
  700.3 1.6 copy.48
  (317 shorter events, 66.2 us)
Async XLA Ops:
  6.5 108.9 %copy-start = (bf16[256,1024]{1,0:T(8,128)(2,1)S(1)}, bf16[256,1024]{1,0:T(8,128)(2,1)}, u32[]{:S(2)}) copy-start(bf16[256,1024]{1,0:T(8,128)(2,1)} %param.13) | copy-start | bytes 1572868
  6.5 355.2 %copy-start.3 = (bf16[16,256]{1,0:T(8,128)(2,1)S(1)}, bf16[16,256]{1,0:T(8,128)(2,1)}, u32[]{:S(2)}) copy-start(bf16[16,256]{1,0:T(8,128)(2,1)} %param.15) | copy-start | bytes 24580
  6.5 473.9 %copy-start.2 = (f32[31,256]{1,0:T(8,128)S(1)}, f32[31,256]{1,0:T(8,128)}, u32[]{:S(2)}) copy-start(f32[31,256]{1,0:T(8,128)} %param.19) | copy-start | bytes 95236
  6.5 474.1 %all-gather.4.cloned.1.call-start = ((), (), s32[]{:S(2)}) async-start(), calls=%async_computation.1 | async-start | bytes 8519680 | tf_op jit(solution)/shard_map/all_gather | solution.py:133
  215.8 342.4 %copy-start.5 = (f32[256]{0:T(256)S(1)}, f32[256]{0:T(256)}, u32[]{:S(2)}) copy-start(f32[256]{0:T(256)} %param.18) | copy-start | bytes 3076
  232.2 0.7 copy-start.1
  232.2 334.4 %copy-start.4 = (bf16[256,16]{0,1:T(8,128)(2,1)S(1)}, bf16[256,16]{0,1:T(8,128)(2,1)}, u32[]{:S(2)}) copy-start(bf16[256,16]{0,1:T(8,128)(2,1)} %param.20) | copy-start | bytes 24580
  232.9 467.4 %reduce-scatter.4.cloned.1.call-start = ((), (), s32[]{:S(2)}) async-start(), calls=%async_computation.2 | async-start | bytes 589824
  558.6 104.7 %collective-permute-start = (bf16[15,256]{1,0:T(8,128)(2,1)S(1)}, bf16[15,256]{1,0:T(8,128)(2,1)S(1)}, u32[]{:S(2)}, u32[]{:S(2)}) collective-permute-start(bf16[15,256]{1,0:T(8,128)(2,1)S(1)} %get-tuple-element.276), channel_id=1, source_target_pairs={{0,8},{8,16},{16,24},{24,32},{32,40},{40,48},{48,56},{56,64},{64,7... | collective-permute-start | bytes 23048 | tf_op jit(solution)/shard_map/ppermute | solution.py:17
  560.5 102.8 %collective-permute-start.1 = (bf16[15,256]{1,0:T(8,128)(2,1)S(1)}, bf16[15,256]{1,0:T(8,128)(2,1)S(1)}, u32[]{:S(2)}, u32[]{:S(2)}) collective-permute-start(bf16[15,256]{1,0:T(8,128)(2,1)S(1)} %get-tuple-element.277), channel_id=1, source_target_pairs={{8,0},{16,8},{24,16},{32,24},{40,32},{48,40},{56,48},{64,56},{72,6... | collective-permute-start | bytes 23048 | tf_op jit(solution)/shard_map/ppermute | solution.py:18
Sparse Core Ops, SparseCore 0:
  233.0 151.7 all-gather.3
  667.5 32.7 reduce-scatter.3
where the time goes:
time: 710 us; the launch traced here: 709 us
  blocking collectives  542 us (76%)
  local copies, waits for them, and re-layouts  85.5 us (12%)
  waiting for transfers between devices  32.9 us (5%)
  other arithmetic  15.8 us (2%)
  between operations  15 us (2%)
  starting transfers between devices  8 us (1%)
    unnamed x1, blocking collectives  122 us
    all_gather x1, blocking collectives, local(): lax.all_gather(z_weight, 'tm', axis=0, tiled=True)  119 us
    all_gather x1, blocking collectives, local(): lax.all_gather(bc_weight, 'tm', axis=0, tiled=True)  107 us
    all_gather x1, blocking collectives, local(): lax.all_gather(x_weight, 'tm', axis=0, tiled=True)  98 us
    all_gather x1, blocking collectives, local(): lax.all_gather(out_weight, 'tm', axis=1, tiled=True)  96.8 us
    dynamic_slice x128, local copies, waits for them, and re-layouts, absorb(): all_summaries[position]  67 us
    unnamed x3, waiting for transfers between devices  32.9 us
  transfers between devices with their start and end apart: 4, of which 1 were waited for; matrix products, arithmetic and copies ran while one was open for 1% of the time, Pallas kernels for 0%

commit v1 on v0

--- a/solution.py
+++ b/solution.py
@@ -99,7 +99,9 @@
     frame_count = frames.shape[0]
     state_width = bc_weight.shape[1] // 2
     pieces = (
-        lax.all_gather(x_weight, "tm", axis=0, tiled=True),
+        jnp.concatenate(
+            lax.all_to_all(jnp.stack([x_weight] * lax.axis_size("tm")), "tm", 0, 0), axis=0
+        ),
         lax.all_gather(z_weight, "tm", axis=0, tiled=True),
         lax.all_gather(bc_weight, "tm", axis=0, tiled=True),
     )

time: 710 us -> 639 us (0.900)
  blocking collectives: 542 us -> 450 us
  starting transfers between devices: 8 us -> 26.8 us
    all_gather x1 -> x0, blocking collectives: 98 us -> none  [local(): lax.all_gather(x_weight, 'tm', axis=0, tiled=True)]
    all_to_all x0 -> x1, starting transfers between devices: none -> 18.7 us  [local(): lax.all_to_all(jnp.stack([x_weight] * lax.axis_size('tm')), 'tm', 0, 0)]
    all_gather x1, blocking collectives: 107 us -> 114 us  [local(): lax.all_gather(bc_weight, 'tm', axis=0, tiled=True)]
  transfers between devices with their start and end apart: 4 -> 5, of which waited for: 1 -> 1; matrix products, arithmetic and copies ran while one was open for 1% -> 2% of each run, Pallas kernels for 0% -> 0%
where the time goes in v1:
time: 639 us; the launch traced here: 637 us
  blocking collectives  450 us (70%)
  local copies, waits for them, and re-layouts  87.1 us (14%)
  waiting for transfers between devices  32.9 us (5%)
  starting transfers between devices  26.8 us (4%)
  other arithmetic  15.8 us (2%)
  between operations  15 us (2%)
  matrix products  6.63 us (1%)
    unnamed x1, blocking collectives  122 us
    all_gather x1, blocking collectives, local(): lax.all_gather(z_weight, 'tm', axis=0, tiled=True)  117 us
    all_gather x1, blocking collectives, local(): lax.all_gather(bc_weight, 'tm', axis=0, tiled=True)  114 us
    all_gather x1, blocking collectives, local(): lax.all_gather(out_weight, 'tm', axis=1, tiled=True)  96.8 us
    dynamic_slice x128, local copies, waits for them, and re-layouts, absorb(): all_summaries[position]  67 us
    unnamed x3, waiting for transfers between devices  32.9 us
    all_to_all x1, starting transfers between devices, local(): lax.all_to_all(jnp.stack([x_weight] * lax.axis_size('tm')), 'tm', 0, 0)  18.7 us
  transfers between devices with their start and end apart: 5, of which 1 were waited for; matrix products, arithmetic and copies ran while one was open for 2% of the time, Pallas kernels for 0%

profile of v1, /device:TPU:8, one launch (start us, length us, event | category | flops | bytes accessed | tf_op | source)
XLA Modules:
  0.0 637.3 jit_solution(10012935831148331063)
XLA Ops:
  6.5 1.6 stack.2
  8.1 18.7 %all-to-all-start = ((bf16[64,16,256]{2,1,0:T(8,128)(2,1)}), bf16[64,16,256]{2,1,0:T(8,128)(2,1)S(1)}, u32[]{:S(2)}, u32[]{:S(2)}) async-start(bf16[64,16,256]{2,1,0:T(8,128)(2,1)} %stack.2), calls=%async_computation | async-start | bytes 1048576 | tf_op jit(solution)/shard_map/all_to_all | solution.py:103
  30.6 114.1 %all_gather.15 = bf16[1024,256]{1,0:T(8,128)(2,1)S(1)} all-gather(bf16[16,256]{1,0:T(8,128)(2,1)} %param.16), channel_id=1, replica_groups=mesh['tm'=64,'head'=8] {'tm'}, dimensions={0}, use_global_device_ids=true | all-gather | bytes 532480 | tf_op jit(solution)/shard_map/all_gather | solution.py:106
  145.7 16.4 %while.27 = (s32[]{:T(128)}, f32[4,128,64]{1,2,0:T(8,128)S(1)}, f32[2,128,4,64]{1,0,3,2:T(2,128)S(1)}, f32[2,4,128]{2,1,0:T(4,128)}, s32[2,128]{1,0:T(2,128)S(1)...) while((s32[]{:T(128)}, f32[4,128,64]{1,2,0:T(8,128)S(1)}, ...), condition=%wide.region_5.6_spmd.clone, body=%wide.region_3.5_spmd.clone.sunk | while | flops 155747840 | bytes 1896203 | solution.py:61
  150.7 2.6 dynamic_update_slice.6
  158.9 2.6 dynamic_update_slice.6
  164.4 1.3 dynamic-slice
  167.2 122.4 %all-reduce = f32[256]{0:T(256)S(1)} all-reduce(f32[256]{0:T(256)S(1)} %multiply_dynamic-update-slice_fusion), channel_id=2, replica_groups=mesh['tm'=64,'head'=8] {'tm'}, use_global_device_ids=true, to_apply=%add | all-reduce | flops 256 | bytes 2048
  290.4 1.2 reduce-window.11
  291.9 116.9 %all_gather.18 = bf16[1024,256]{1,0:T(8,128)(2,1)S(1)} all-gather(bf16[16,256]{1,0:T(8,128)(2,1)S(1)} %copy-done.3), channel_id=1, replica_groups=mesh['tm'=64,'head'=8] {'tm'}, dimensions={0}, use_global_device_ids=true | all-gather | bytes 532480 | tf_op jit(solution)/shard_map/all_gather | solution.py:105
  409.2 77.0 %while.28 = (s32[]{:T(128)}, f32[4,128,64]{2,1,0:T(8,128)S(1)}, s32[]{:T(128)}, f32[64,4]{1,0:T(8,128)S(1)}, f32[64,4,128,64]{2,3,1,0:T(8,128)}, /*index=5*/s32[]{:T(128)}, s32[]{:T(128)}) while((s32[]{:T(128)}, f32[4,128,64]{2,1,0:T(8,128)S(1)}, s32[]{:T(128)}, f32[64,4]{1,0:T(8,128)S(1)}, f32[64,4,128,64]{2,3,1,0:T(8,128)}, ...), condition=%wide.region_8.9_spmd.clone, body=%wide.region_7.8_spmd.clone.sunk | while | flops 131076 | bytes 917657 | solution.py:143
  409.3 0.9 constant_dynamic-slice_fusion.4
  410.5 0.9 constant_dynamic-slice_fusion.4
  411.7 0.9 constant_dynamic-slice_fusion.4
  412.9 0.9 constant_dynamic-slice_fusion.4
  417.7 0.9 constant_dynamic-slice_fusion.4
  418.9 0.9 constant_dynamic-slice_fusion.4
  420.1 0.9 constant_dynamic-slice_fusion.4
  421.3 0.9 constant_dynamic-slice_fusion.4
  422.5 0.9 constant_dynamic-slice_fusion.4
  423.7 0.9 constant_dynamic-slice_fusion.4
  424.9 0.9 constant_dynamic-slice_fusion.4
  428.5 0.9 constant_dynamic-slice_fusion.4
  429.7 0.9 constant_dynamic-slice_fusion.4
  430.9 0.9 constant_dynamic-slice_fusion.4
  432.1 0.9 constant_dynamic-slice_fusion.4
  433.3 0.9 constant_dynamic-slice_fusion.4
  434.5 0.9 constant_dynamic-slice_fusion.4
  435.7 0.9 constant_dynamic-slice_fusion.4
  440.5 0.9 constant_dynamic-slice_fusion.4
  441.7 0.9 constant_dynamic-slice_fusion.4
  442.9 0.9 constant_dynamic-slice_fusion.4
  444.1 0.9 constant_dynamic-slice_fusion.4
  445.4 0.9 constant_dynamic-slice_fusion.4
  446.6 0.9 constant_dynamic-slice_fusion.4
  447.8 0.9 constant_dynamic-slice_fusion.4
  451.4 0.9 constant_dynamic-slice_fusion.4
  452.6 0.9 constant_dynamic-slice_fusion.4
  453.8 0.9 constant_dynamic-slice_fusion.4
  455.0 0.9 constant_dynamic-slice_fusion.4
  456.2 0.9 constant_dynamic-slice_fusion.4
  487.2 1.9 collective-permute-start
  489.1 6.0 collective-permute-start.1
  495.2 96.8 %all_gather.19 = bf16[256,1024]{0,1:T(8,128)(2,1)S(1)} all-gather(bf16[256,16]{0,1:T(8,128)(2,1)S(1)} %copy-done.4), channel_id=1, replica_groups=mesh['tm'=64,'head'=8] {'tm'}, dimensions={1}, use_global_device_ids=true | all-gather | bytes 532480 | tf_op jit(solution)/shard_map/all_gather | solution.py:165
  592.0 3.0 convolution_convert_fusion
  595.0 1.0 copy.47
  596.0 32.9 %reduce-scatter.4.cloned.1.call-done = bf16[128,256]{1,0:T(8,128)(2,1)} async-done(((bf16[1024,256]{1,0:T(8,128)(2,1)}), bf16[128,256]{1,0:T(8,128)(2,1)}) %reduce-scatter.4.cloned.1.call-update) | async-done | bytes 65552
  628.9 1.6 copy.48
  (319 shorter events, 67.1 us)
Async XLA Ops:
  6.5 138.2 %copy-start = (bf16[256,1024]{1,0:T(8,128)(2,1)S(1)}, bf16[256,1024]{1,0:T(8,128)(2,1)}, u32[]{:S(2)}) copy-start(bf16[256,1024]{1,0:T(8,128)(2,1)} %param.13) | copy-start | bytes 1572868
  6.5 285.3 %copy-start.3 = (bf16[16,256]{1,0:T(8,128)(2,1)S(1)}, bf16[16,256]{1,0:T(8,128)(2,1)}, u32[]{:S(2)}) copy-start(bf16[16,256]{1,0:T(8,128)(2,1)} %param.15) | copy-start | bytes 24580
  6.5 402.3 %copy-start.2 = (f32[31,256]{1,0:T(8,128)S(1)}, f32[31,256]{1,0:T(8,128)}, u32[]{:S(2)}) copy-start(f32[31,256]{1,0:T(8,128)} %param.19) | copy-start | bytes 95236
  8.1 136.9 %all-to-all-start = ((bf16[64,16,256]{2,1,0:T(8,128)(2,1)}), bf16[64,16,256]{2,1,0:T(8,128)(2,1)S(1)}, u32[]{:S(2)}, u32[]{:S(2)}) async-start(bf16[64,16,256]{2,1,0:T(8,128)(2,1)} %stack.2), calls=%async_computation | async-start | bytes 1048576 | tf_op jit(solution)/shard_map/all_to_all | solution.py:103
  26.9 382.4 %all-gather.4.cloned.1.call-start = ((), (), s32[]{:S(2)}) async-start(), calls=%async_computation.2 | async-start | bytes 8519680 | tf_op jit(solution)/shard_map/all_gather | solution.py:135
  145.7 341.2 %copy-start.5 = (f32[256]{0:T(256)S(1)}, f32[256]{0:T(256)}, u32[]{:S(2)}) copy-start(f32[256]{0:T(256)} %param.18) | copy-start | bytes 3076
  162.1 0.7 copy-start.1
  162.1 333.1 %copy-start.4 = (bf16[256,16]{0,1:T(8,128)(2,1)S(1)}, bf16[256,16]{0,1:T(8,128)(2,1)}, u32[]{:S(2)}) copy-start(bf16[256,16]{0,1:T(8,128)(2,1)} %param.20) | copy-start | bytes 24580
  162.7 466.1 %reduce-scatter.4.cloned.1.call-start = ((), (), s32[]{:S(2)}) async-start(), calls=%async_computation.3 | async-start | bytes 589824
  487.2 104.7 %collective-permute-start = (bf16[15,256]{1,0:T(8,128)(2,1)S(1)}, bf16[15,256]{1,0:T(8,128)(2,1)S(1)}, u32[]{:S(2)}, u32[]{:S(2)}) collective-permute-start(bf16[15,256]{1,0:T(8,128)(2,1)S(1)} %get-tuple-element.276), channel_id=1, source_target_pairs={{0,8},{8,16},{16,24},{24,32},{32,40},{40,48},{48,56},{56,64},{64,7... | collective-permute-start | bytes 23048 | tf_op jit(solution)/shard_map/ppermute | solution.py:17
  489.1 102.8 %collective-permute-start.1 = (bf16[15,256]{1,0:T(8,128)(2,1)S(1)}, bf16[15,256]{1,0:T(8,128)(2,1)S(1)}, u32[]{:S(2)}, u32[]{:S(2)}) collective-permute-start(bf16[15,256]{1,0:T(8,128)(2,1)S(1)} %get-tuple-element.277), channel_id=1, source_target_pairs={{8,0},{16,8},{24,16},{32,24},{40,32},{48,40},{56,48},{64,56},{72,6... | collective-permute-start | bytes 23048 | tf_op jit(solution)/shard_map/ppermute | solution.py:18
Sparse Core Ops, SparseCore 0:
  162.9 154.1 all-gather.3
  596.1 32.7 reduce-scatter.3
